TPU v7x, 32 devices: a whole 2x2x4 slice. The times are simulated.
32 devices in a mesh: leaf: 16 (over z, y, x), col: 2 (over core).
Axes of the slice: x: 2, y: 2, z: 4, core: 2. Of those that a mesh axis runs over, the one named last changes fastest.
Arguments:
- sources: bfloat16 [65536, 256], P('leaf', 'col'), may hold values from -6 to 6
- near_tiles: bfloat16 [256, 8, 256, 256], P('leaf', 'col'), may hold values from -0.125 to 0.125
- near_index: int32 [256, 8], P('leaf'), may hold values from 0 to 255, as said below
- near_count: int32 [256], P('leaf'), may hold values from 1 to 8, as said below
- leaf_basis: bfloat16 [256, 64, 256], P('leaf'), may hold values from -0.375 to 0.375
- leaf_coupling: bfloat16 [256, 64, 256], P('leaf'), may hold values from -0.375 to 0.375
- leaf_far: int32 [256, 4], P('leaf'), may hold values from 0 to 255, as said below
- up_leaf: bfloat16 [32, 64, 512], P('leaf'), may hold values from -0.25 to 0.25
- mid_coupling: bfloat16 [32, 64, 256], P('leaf'), may hold values from -0.375 to 0.375
- mid_far: int32 [32, 4], P('leaf'), may hold values from 0 to 31, as said below
- up_mid: bfloat16 [32, 64, 64], P('leaf'), may hold values from -0.75 to 0.75
- top_coupling: bfloat16 [4, 64, 256], replicated, may hold values from -0.4375 to 0.4375
Outputs:
- product: float32 [65536, 256], P('leaf', 'col')
Inputs may be any that keep to these rules, and one draw needn't show every extreme that they name: `near_index`: entry 0 of row i is i; the other 7 entries are distinct leaves j with j != i and |i - j| <= 8. Only the first near_count[i] slots of leaf i count; some leaf has all 8. `leaf_far`: row i holds 4 distinct leaves j != i with |i // 8 - j // 8| <= 1. `mid_far`: row a holds 4 distinct middle clusters b != a with |a // 8 - b // 8| <= 1.
All inputs are finite; a program needn't handle non-finite values.
Results may differ from a plain program's by a relative error of at most 0.01.
Values may be sent and summed in bfloat16 or wider, within the bound.
No kernel may reach another device: no remote copies, remote signals or barrier semaphores. Data moves between devices by JAX's collectives and lax.ppermute only.
A program may use at most 128 MiB of HBM per device.

v0:
```python
import jax
import jax.numpy as jnp
from jax import lax
from jax.sharding import PartitionSpec as P

CHILD = 8
FAR = 4


def padded(x, sides, width):
    for axis, dim in sides:
        size, length = (lax.axis_size(axis), x.shape[dim])
        up = [(i, (i + 1) % size) for i in range(size - 1)]
        down = [(j, i) for i, j in up]
        last = lax.slice_in_dim(x, length - width, length, axis=dim)
        first = lax.slice_in_dim(x, 0, width, axis=dim)
        before = lax.ppermute(last, axis, up)
        after = lax.ppermute(first, axis, down)
        x = jnp.concatenate([before, x, after], axis=dim)
    return x


def shards(
    sources,
    near_tiles,
    near_index,
    near_count,
    leaf_basis,
    leaf_coupling,
    leaf_far,
    up_leaf,
    mid_coupling,
    mid_far,
    up_mid,
    top_coupling,
):
    f32 = jnp.float32
    bf16 = jnp.bfloat16
    leaf_count = leaf_basis.shape[0]
    rank_size = leaf_basis.shape[1]
    leaf_size = leaf_basis.shape[2]
    col_count = sources.shape[1]
    mid_count = leaf_count // CHILD
    total_top = top_coupling.shape[0]
    device = lax.axis_index("leaf")
    first_leaf = device * leaf_count
    first_mid = device * mid_count
    window = padded(sources, (("leaf", 0),), CHILD * leaf_size)
    near_local = near_index - (first_leaf - CHILD)
    all_tiles = lax.all_gather(near_tiles, "col", axis=1, tiled=True)
    slot_count = all_tiles.shape[1]
    blocks = window.reshape(-1, leaf_size, window.shape[1])
    picked = blocks[near_local]
    live_mask = jnp.arange(slot_count)[None, :] < near_count[:, None]
    picked = jnp.where(live_mask[:, :, None, None], picked, jnp.zeros((), bf16))
    result = jnp.einsum("lsij,lsjc->lic", all_tiles, picked, preferred_element_type=f32)
    near_part = result.reshape(leaf_count * leaf_size, window.shape[1])
    leaf_blocks = sources.reshape(leaf_count, leaf_size, col_count)
    leaf_coef = jnp.einsum(
        "lrk,lkc->lrc", leaf_basis, leaf_blocks, preferred_element_type=f32
    ).astype(bf16)
    mid_coef = jnp.einsum(
        "qrk,qkc->qrc",
        up_leaf,
        leaf_coef.reshape(mid_count, CHILD * rank_size, col_count),
        preferred_element_type=f32,
    ).astype(bf16)
    mid_lift = jnp.einsum("qrs,qsc->qrc", up_mid, mid_coef, preferred_element_type=f32).astype(bf16)
    parent = (first_mid + jnp.arange(mid_count)) // CHILD
    mid_flat = mid_far.reshape(-1)
    top_range = jnp.arange(total_top)
    coef_piece = lax.all_gather(mid_coef, "leaf", axis=0, tiled=True)
    lift_piece = lax.all_gather(mid_lift, "leaf", axis=0, tiled=True)
    global_ids = jnp.arange(coef_piece.shape[0])
    group_map = (top_range[:, None] == (global_ids // CHILD)[None, :]).astype(bf16)
    top_total = jnp.einsum("pk,krc->prc", group_map, lift_piece, preferred_element_type=f32)
    global_ids = jnp.arange(coef_piece.shape[0])
    pick_map = (mid_flat[:, None] == global_ids[None, :]).astype(bf16)
    mid_picked = jnp.einsum("ik,krc->irc", pick_map, coef_piece, preferred_element_type=f32)
    top_coef = top_total.astype(bf16)
    parent_rows = top_coupling[parent]
    keep_mask = top_range[None, :] != parent[:, None]
    stacked = jnp.where(keep_mask[:, :, None, None], top_coef[None], jnp.zeros((), bf16))
    top_field = jnp.einsum(
        "qrk,qkc->qrc",
        parent_rows,
        stacked.reshape(mid_count, total_top * rank_size, col_count),
        preferred_element_type=f32,
    ).astype(bf16)
    mid_chosen = mid_picked.astype(bf16).reshape(mid_count, FAR * rank_size, col_count)
    mid_field = (
        jnp.einsum("qrk,qkc->qrc", mid_coupling, mid_chosen, preferred_element_type=f32)
        + jnp.einsum("qrs,qrc->qsc", up_mid, top_field, preferred_element_type=f32)
    ).astype(bf16)
    leaf_window = padded(leaf_coef, (("leaf", 0),), CHILD)
    far_local = leaf_far - (first_leaf - CHILD)
    leaf_chosen = leaf_window[far_local].reshape(leaf_count, FAR * rank_size, col_count)
    down_part = jnp.einsum("qrs,qrc->qsc", up_leaf, mid_field, preferred_element_type=f32).reshape(
        leaf_count, rank_size, col_count
    )
    leaf_field = (
        jnp.einsum("lrk,lkc->lrc", leaf_coupling, leaf_chosen, preferred_element_type=f32)
        + down_part
    ).astype(bf16)
    far_part = jnp.einsum(
        "lrk,lrc->lkc", leaf_basis, leaf_field, preferred_element_type=f32
    ).reshape(leaf_count * leaf_size, col_count)
    return near_part + far_part


def solution(mesh):
    return jax.shard_map(
        shards,
        mesh=mesh,
        in_specs=(
            P("leaf", "col"),
            P("leaf", "col", None, None),
            P("leaf", None),
            P("leaf"),
            P("leaf", None, None),
            P("leaf", None, None),
            P("leaf", None),
            P("leaf", None, None),
            P("leaf", None, None),
            P("leaf", None),
            P("leaf", None, None),
            P(),
        ),
        out_specs=P("leaf", "col"),
        check_vma=False,
    )
```

profile of v0, /device:TPU:0, one launch (start us, length us, event | category | flops | bytes accessed | tf_op | source)
XLA Modules:
  0.0 168.7 jit_solution(13844385451105794318)
XLA Ops:
  6.5 0.0 copy-start
  6.5 0.0 copy-start.1
  6.5 0.0 all-gather.2.cloned.1.call-start
  6.5 0.7 all-gather.2.cloned.1.call-update
  7.3 0.0 copy-start.9
  7.3 0.0 copy-start.4
  7.3 0.0 copy-start.6
  7.3 0.0 copy-start.11
  7.3 0.0 copy-start.7
  7.3 0.0 copy-start.10
  7.3 0.0 copy-start.8
  7.3 0.0 copy-start.5
  7.3 0.2 copy-done
  7.6 0.3 copy-done.1
  7.9 0.3 convolution_convert_fusion
  8.3 4.9 %collective-permute-start.2 = (bf16[8,64,128]{2,1,0:T(8,128)(2,1)S(1)}, bf16[8,64,128]{2,1,0:T(8,128)(2,1)S(1)}, u32[]{:S(2)}, u32[]{:S(2)}) collective-permute-start(bf16[8,64,128]{2,1,0:T(8,128)(2,1)S(1)} %get-tuple-element.7), channel_id=1, source_target_pairs={{0,2},{2,4},{4,6},{6,8},{8,10},{10,12},{12,14},{14,16},{16,18},{18... | collective-permute-start | bytes 393224 | tf_op jit(solution)/shard_map/ppermute | solution.py:17
  13.2 1.3 collective-permute-start.3
  14.5 1.1 fusion.33
  15.5 5.4 %collective-permute-start = (bf16[2048,128]{1,0:T(8,128)(2,1)}, bf16[2048,128]{1,0:T(8,128)(2,1)}, u32[]{:S(2)}, u32[]{:S(2)}) collective-permute-start(bf16[2048,128]{1,0:T(8,128)(2,1)} %get-tuple-element.5), channel_id=1, source_target_pairs={{0,2},{2,4},{4,6},{6,8},{8,10},{10,12},{12,14},{14,16},{16,18},{18... | collective-permute-start | bytes 1572872 | tf_op jit(solution)/shard_map/ppermute | solution.py:17
  20.9 1.3 collective-permute-start.1
  22.2 0.0 copy-done.9
  22.2 0.1 copy.27
  22.3 0.1 reshape.160
  22.4 0.0 copy-done.4
  22.4 0.2 convolution_convert_fusion.5
  22.6 0.0 copy-done.6
  22.6 0.1 fusion.12
  22.7 0.0 copy-start.3
  22.7 57.8 %all_gather.11 = bf16[32,64,128]{2,1,0:T(8,128)(2,1)S(1)} all-gather(bf16[2,64,128]{2,1,0:T(8,128)(2,1)S(1)} %fusion.12), channel_id=1, replica_groups=mesh['leaf'=16,'col'=2] {'leaf'}, dimensions={0}, use_global_device_ids=true | all-gather | bytes 557056 | tf_op jit(solution)/shard_map/all_gather | solution.py:73
  80.5 0.4 convolution_convert_fusion.2
  80.9 0.1 iota_compare_fusion.3
  81.0 0.1 broadcast_in_dim.59
  81.1 0.1 broadcast_in_dim.60
  81.2 0.0 copy-done.11
  81.2 0.1 eq.28
  81.3 38.7 %all_gather.10 = bf16[32,64,128]{2,1,0:T(8,128)(2,1)S(1)} all-gather(bf16[2,64,128]{2,1,0:T(8,128)(2,1)S(1)} %bitcast.59), channel_id=1, replica_groups=mesh['leaf'=16,'col'=2] {'leaf'}, dimensions={0}, use_global_device_ids=true | all-gather | bytes 557056 | tf_op jit(solution)/shard_map/all_gather | solution.py:72
  119.9 0.4 convolution_convert_fusion.1
  120.4 0.0 copy-done.7
  120.4 0.6 gather_fusion.2
  121.0 0.0 copy-done.10
  121.0 0.1 iota_compare_fusion
  121.1 0.0 copy-done.8
  121.1 0.4 fusion.11
  121.5 0.0 copy-done.5
  121.5 0.4 convolution_bitcast_fusion.1
  121.9 0.1 copy.25
  122.0 0.1 reshape.152
  122.1 0.2 copy.33
  122.3 0.0 collective-permute-done.2
  122.3 0.0 collective-permute-done.3
  122.3 1.0 pad_maximum_fusion.1
  123.3 0.7 gather_fusion.1
  124.0 0.0 copy-done.3
  124.0 1.9 %fusion.9 = f32[16,128,256]{2,1,0:T(8,128)} fusion(bf16[16,64,256]{2,1,0:T(8,128)(2,1)S(1)} %copy-done, f32[16,64,128]{2,1,0:T(8,128)S(1)} %bitcast.57, bf16[16,64,256]{2,1,0:T(8,128)(2,1)S(1)} %copy-done.3, bf16[16,256,128]{2,1,0:T(8,128)(2,1)S(1)} %bitcast.56), kind=kOutput, calls=%fused_computation.15 | convolution fusion | flops 134479872 | bytes 4718592 | tf_op jit(solution)/shard_map/lrk,lrc->lkc/dot_general | solution.py:105
  126.0 0.0 collective-permute-done
  126.0 0.0 collective-permute-done.1
  126.0 1.7 pad_maximum_fusion
  127.6 6.6 %gather_fusion = bf16[128,256,128]{2,1,0:T(8,128)(2,1)} fusion(bf16[32,256,128]{2,1,0:T(8,128)(2,1)S(1)} %bitcast.52, s32[1024]{0:T(1024)S(1)} %pad_clamp_fusion.2), kind=kCustom, calls=%fused_computation | custom fusion | bytes 16777728 | tf_op jit(solution)/shard_map/gather | solution.py:53
  134.2 0.0 copy-start.2
  134.2 12.1 %copy.26 = bf16[128,256,128]{1,2,0:T(8,128)(2,1)} copy(bf16[128,256,128]{2,1,0:T(8,128)(2,1)} %gather_fusion) | data formatting | bytes 16777216 | tf_op jit(solution)/shard_map/gather | solution.py:53
  146.3 0.0 all-gather.2.cloned.1.call-done
  146.3 0.0 copy-done.2
  146.3 12.7 %fusion.4 = f32[16,256,128]{1,2,0:T(8,128)} fusion(f32[16,128,256]{2,1,0:T(8,128)S(1)} %copy-done.2, bf16[16,8,256,256]{3,2,1,0:T(8,128)(2,1)} %all-gather.2.cloned.1.call-done, bf16[16,8,256,128]{2,3,1,0:T(8,128)(2,1)} %bitcast.54, pred[16,8]{1,0:T(8,128)(4,1)S(1)} %iota_compare_fusion), kind=kOutput, calls=%fused_computation.9 | convolution fusion | flops 2152202240 | bytes 29360256 | tf_op jit(solution)/shard_map/lsij,lsjc->lic/dot_general | solution.py:56
  159.0 2.9 %copy.34 = f32[16,256,128]{2,1,0:T(8,128)} copy(f32[16,256,128]{1,2,0:T(8,128)} %fusion.4) | data formatting | bytes 4194304 | tf_op jit(solution)/shard_map/add | solution.py:108
  (11 shorter events, 0.1 us)
Async XLA Ops:
  6.5 1.0 copy-start
  6.5 1.4 copy-start.1
  6.5 139.8 %all-gather.2.cloned.1.call-start = ((), (), s32[]{:S(2)}) async-start(), calls=%async_computation | async-start | bytes 25165824 | tf_op jit(solution)/shard_map/all_gather | solution.py:50
  7.3 14.9 %copy-start.9 = (s32[16,4]{0,1:T(4,128)S(1)}, s32[16,4]{0,1:T(4,128)}, u32[]{:S(2)}) copy-start(s32[16,4]{0,1:T(4,128)} %param.18) | copy-start | bytes 772
  7.3 15.1 %copy-start.4 = (bf16[2,64,512]{2,1,0:T(8,128)(2,1)S(1)}, bf16[2,64,512]{2,1,0:T(8,128)(2,1)}, u32[]{:S(2)}) copy-start(bf16[2,64,512]{2,1,0:T(8,128)(2,1)} %param.19) | copy-start | bytes 393220
  7.3 15.3 %copy-start.6 = (bf16[2,64,64]{2,1,0:T(8,128)(2,1)S(1)}, bf16[2,64,64]{2,1,0:T(8,128)(2,1)}, u32[]{:S(2)}) copy-start(bf16[2,64,64]{2,1,0:T(8,128)(2,1)} %param.22) | copy-start | bytes 49156
  7.3 73.9 %copy-start.11 = (s32[2,4]{1,0:T(2,128)S(1)}, s32[2,4]{1,0:T(2,128)}, u32[]{:S(2)}) copy-start(s32[2,4]{1,0:T(2,128)} %param.21) | copy-start | bytes 100
  7.3 113.1 %copy-start.7 = (bf16[4,64,256]{2,1,0:T(8,128)(2,1)S(1)}, bf16[4,64,256]{2,1,0:T(8,128)(2,1)}, u32[]{:S(2)}) copy-start(bf16[4,64,256]{2,1,0:T(8,128)(2,1)} %param.23) | copy-start | bytes 393220
  7.3 113.7 %copy-start.10 = (s32[16]{0:T(128)S(1)}, s32[16]{0:T(128)}, u32[]{:S(2)}) copy-start(s32[16]{0:T(128)} %param.15) | copy-start | bytes 196
  7.3 113.7 %copy-start.8 = (s32[16,8]{0,1:T(8,128)S(1)}, s32[16,8]{0,1:T(8,128)}, u32[]{:S(2)}) copy-start(s32[16,8]{0,1:T(8,128)} %param.14) | copy-start | bytes 1540
  7.3 114.1 %copy-start.5 = (bf16[2,64,256]{2,1,0:T(8,128)(2,1)S(1)}, bf16[2,64,256]{2,1,0:T(8,128)(2,1)}, u32[]{:S(2)}) copy-start(bf16[2,64,256]{2,1,0:T(8,128)(2,1)} %param.20) | copy-start | bytes 196612
  8.3 114.0 %collective-permute-start.2 = (bf16[8,64,128]{2,1,0:T(8,128)(2,1)S(1)}, bf16[8,64,128]{2,1,0:T(8,128)(2,1)S(1)}, u32[]{:S(2)}, u32[]{:S(2)}) collective-permute-start(bf16[8,64,128]{2,1,0:T(8,128)(2,1)S(1)} %get-tuple-element.7), channel_id=1, source_target_pairs={{0,2},{2,4},{4,6},{6,8},{8,10},{10,12},{12,14},{14,16},{16,18},{18... | collective-permute-start | bytes 393224 | tf_op jit(solution)/shard_map/ppermute | solution.py:17
  13.2 109.1 %collective-permute-start.3 = (bf16[8,64,128]{2,1,0:T(8,128)(2,1)S(1)}, bf16[8,64,128]{2,1,0:T(8,128)(2,1)}, u32[]{:S(2)}, u32[]{:S(2)}) collective-permute-start(bf16[8,64,128]{2,1,0:T(8,128)(2,1)S(1)} %get-tuple-element.8), channel_id=1, source_target_pairs={{2,0},{4,2},{6,4},{8,6},{10,8},{12,10},{14,12},{16,14},{18,16},{20... | collective-permute-start | bytes 393224 | tf_op jit(solution)/shard_map/ppermute | solution.py:18
  15.5 110.4 %collective-permute-start = (bf16[2048,128]{1,0:T(8,128)(2,1)}, bf16[2048,128]{1,0:T(8,128)(2,1)}, u32[]{:S(2)}, u32[]{:S(2)}) collective-permute-start(bf16[2048,128]{1,0:T(8,128)(2,1)} %get-tuple-element.5), channel_id=1, source_target_pairs={{0,2},{2,4},{4,6},{6,8},{8,10},{10,12},{12,14},{14,16},{16,18},{18... | collective-permute-start | bytes 1572872 | tf_op jit(solution)/shard_map/ppermute | solution.py:17
  20.9 105.1 %collective-permute-start.1 = (bf16[2048,128]{1,0:T(8,128)(2,1)}, bf16[2048,128]{1,0:T(8,128)(2,1)}, u32[]{:S(2)}, u32[]{:S(2)}) collective-permute-start(bf16[2048,128]{1,0:T(8,128)(2,1)} %get-tuple-element.6), channel_id=1, source_target_pairs={{2,0},{4,2},{6,4},{8,6},{10,8},{12,10},{14,12},{16,14},{18,16},{20... | collective-permute-start | bytes 1572872 | tf_op jit(solution)/shard_map/ppermute | solution.py:18
  22.7 101.3 %copy-start.3 = (bf16[16,64,256]{2,1,0:T(8,128)(2,1)S(1)}, bf16[16,64,256]{2,1,0:T(8,128)(2,1)}, u32[]{:S(2)}) copy-start(bf16[16,64,256]{2,1,0:T(8,128)(2,1)} %param.17) | copy-start | bytes 1572868
  134.2 12.1 %copy-start.2 = (f32[16,128,256]{2,1,0:T(8,128)S(1)}, f32[16,128,256]{2,1,0:T(8,128)}, u32[]{:S(2)}) copy-start(f32[16,128,256]{2,1,0:T(8,128)} %fusion.9) | copy-start | bytes 6291460
Sparse Core Ops, SparseCore 0:
  8.9 32.7 all-gather.1
where the time goes:
time: 169 us
  blocking collectives  96.5 us (57%)
  local copies, waits for them, and re-layouts  25.4 us (15%)
  matrix products  16.8 us (10%)
  between operations  13.7 us (8%)
  starting transfers between devices  12.8 us (8%)
  other arithmetic  2.82 us (2%)
    all_gather x1, blocking collectives, shards(): lift_piece = lax.all_gather(mid_lift, 'leaf', axis=0, tiled=True)  57.8 us
    all_gather x1, blocking collectives, shards(): coef_piece = lax.all_gather(mid_coef, 'leaf', axis=0, tiled=True)  38.7 us
    gather x2, local copies, waits for them, and re-layouts, shards(): picked = blocks[near_local]  18.7 us
    dot_general x1, matrix products, shards(): jnp.einsum('lsij,lsjc->lic', all_tiles, picked, preferred_element_type=f32)  12.7 us
    ppermute x2, starting transfers between devices, padded(): before = lax.ppermute(last, axis, up)  10.2 us
  transfers between devices with their start and end apart: 5, of which 0 were waited for; matrix products, arithmetic and copies ran while one was open for 17% of the time, Pallas kernels for 0%

commit v1 on v0

--- a/solution.py
+++ b/solution.py
@@ -70,7 +70,15 @@
     mid_flat = mid_far.reshape(-1)
     top_range = jnp.arange(total_top)
     coef_piece = lax.all_gather(mid_coef, "leaf", axis=0, tiled=True)
-    lift_piece = lax.all_gather(mid_lift, "leaf", axis=0, tiled=True)
+    ways, here, step = (lax.axis_size("leaf"), lax.axis_index("leaf"), mid_lift.shape[0])
+    line, have = (mid_lift, 1)
+    while have < ways:
+        line = jnp.concatenate(
+            [line, lax.ppermute(line, "leaf", [(d, (d - have) % ways) for d in range(ways)])],
+            axis=0,
+        )
+        have = 2 * have
+    lift_piece = jnp.roll(line, here * step, axis=0)
     global_ids = jnp.arange(coef_piece.shape[0])
     group_map = (top_range[:, None] == (global_ids // CHILD)[None, :]).astype(bf16)
     top_total = jnp.einsum("pk,krc->prc", group_map, lift_piece, preferred_element_type=f32)

time: 169 us -> 158 us (0.935)
  blocking collectives: 96.5 us -> 54.9 us
  waiting for transfers between devices: 0.72 us -> 14.5 us
  local copies, waits for them, and re-layouts: 25.4 us -> 33.7 us
  starting transfers between devices: 12.8 us -> 16.3 us
  matrix products: 16.8 us -> 19.7 us
    all_gather x1 -> x0, blocking collectives: 57.8 us -> none  [shards(): lift_piece = lax.all_gather(mid_lift, 'leaf', axis=0, tiled=True)]
    all_gather x1, blocking collectives: 38.7 us -> 54.9 us  [shards(): coef_piece = lax.all_gather(mid_coef, 'leaf', axis=0, tiled=True)]
    ppermute x0 -> x4, waiting for transfers between devices: none -> 13.8 us  [shards(): lax.ppermute(line, 'leaf', [(d, (d - have) % ways) for d in range(ways)])]
    ppermute x0 -> x4, starting transfers between devices: none -> 7.08 us  [shards(): lax.ppermute(line, 'leaf', [(d, (d - have) % ways) for d in range(ways)])]
    unnamed x24 -> x34, local copies, waits for them, and re-layouts: 0.63 us -> 5.82 us
    ppermute x2, starting transfers between devices: 10.2 us -> 6.63 us  [padded(): before = lax.ppermute(last, axis, up)]
  transfers between devices with their start and end apart: 5 -> 9, of which waited for: 0 -> 3; matrix products, arithmetic and copies ran while one was open for 17% -> 26% of each run, Pallas kernels for 0% -> 0%
where the time goes in v1:
time: 158 us; the launch traced here: 157 us
  blocking collectives  54.9 us (35%)
  local copies, waits for them, and re-layouts  33.7 us (21%)
  matrix products  19.7 us (12%)
  starting transfers between devices  16.3 us (10%)
  waiting for transfers between devices  14.5 us (9%)
  between operations  13.7 us (9%)
  other arithmetic  4.17 us (3%)
    all_gather x1, blocking collectives, shards(): coef_piece = lax.all_gather(mid_coef, 'leaf', axis=0, tiled=True)  54.9 us
    gather x2, local copies, waits for them, and re-layouts, shards(): picked = blocks[near_local]  18.7 us
    ppermute x4, waiting for transfers between devices, shards(): lax.ppermute(line, 'leaf', [(d, (d - have) % ways) for d in range(ways)])  13.8 us
    dot_general x1, matrix products, shards(): jnp.einsum('lsij,lsjc->lic', all_tiles, picked, preferred_element_type=f32)  12.7 us
    ppermute x4, starting transfers between devices, shards(): lax.ppermute(line, 'leaf', [(d, (d - have) % ways) for d in range(ways)])  7.08 us
    ppermute x2, starting transfers between devices, padded(): before = lax.ppermute(last, axis, up)  6.63 us
    unnamed x34, local copies, waits for them, and re-layouts  5.82 us
  transfers between devices with their start and end apart: 9, of which 3 were waited for; matrix products, arithmetic and copies ran while one was open for 26% of the time, Pallas kernels for 0%

profile of v1, /device:TPU:0, one launch (start us, length us, event | category | flops | bytes accessed | tf_op | source)
XLA Modules:
  0.0 157.0 jit_solution(36829596399399992)
XLA Ops:
  6.5 0.0 all-gather.2.cloned.1.call-start
  6.6 0.7 all-gather.2.cloned.1.call-update
  7.3 0.3 copy-done
  7.6 0.3 copy-done.1
  7.9 0.3 convolution_convert_fusion
  8.3 0.2 convolution_convert_fusion.5
  8.4 0.7 constant_dynamic-update-slice_fusion.9
  9.2 7.0 %collective-permute-start.4 = (bf16[2,64,128]{2,1,0:T(8,128)(2,1)S(1)}, bf16[2,64,128]{2,1,0:T(8,128)(2,1)S(1)}, u32[]{:S(2)}, u32[]{:S(2)}) collective-permute-start(bf16[2,64,128]{2,1,0:T(8,128)(2,1)S(1)} %get-tuple-element.10), channel_id=1, source_target_pairs={{0,30},{2,0},{4,2},{6,4},{8,6},{10,8},{12,10},{14,12},{16,14},{18,... | collective-permute-start | bytes 98312 | tf_op jit(solution)/shard_map/ppermute | solution.py:77
  16.2 1.3 collective-permute-start.2
  17.5 1.3 collective-permute-start.3
  18.8 1.1 fusion.33
  19.9 5.3 %collective-permute-start = (bf16[2048,128]{1,0:T(8,128)(2,1)}, bf16[2048,128]{1,0:T(8,128)(2,1)}, u32[]{:S(2)}, u32[]{:S(2)}) collective-permute-start(bf16[2048,128]{1,0:T(8,128)(2,1)} %get-tuple-element.5), channel_id=1, source_target_pairs={{0,2},{2,4},{4,6},{6,8},{8,10},{10,12},{12,14},{14,16},{16,18},{18... | collective-permute-start | bytes 1572872 | tf_op jit(solution)/shard_map/ppermute | solution.py:17
  25.2 1.3 collective-permute-start.1
  26.5 0.1 eq.31
  26.6 0.0 copy-done.10
  26.6 0.1 copy.29
  26.7 0.1 reshape.160
  26.8 0.1 iota_compare_fusion.3
  26.9 0.1 iota_compare_fusion
  27.0 54.9 %all_gather.7 = bf16[32,64,128]{2,1,0:T(8,128)(2,1)S(1)} all-gather(bf16[2,64,128]{2,1,0:T(8,128)(2,1)S(1)} %bitcast.59), channel_id=1, replica_groups=mesh['leaf'=16,'col'=2] {'leaf'}, dimensions={0}, use_global_device_ids=true | all-gather | bytes 557056 | tf_op jit(solution)/shard_map/all_gather | solution.py:72
  81.9 0.4 convolution_convert_fusion.1
  82.3 0.1 copy.27
  82.4 0.1 reshape.152
  82.5 0.0 collective-permute-done.4
  82.5 0.1 collective-permute-start.5
  82.6 4.2 %collective-permute-done.5 = bf16[4,64,128]{2,1,0:T(8,128)(2,1)S(1)} collective-permute-done((bf16[4,64,128]{2,1,0:T(8,128)(2,1)S(1)}, bf16[4,64,128]{2,1,0:T(8,128)(2,1)S(1)}, u32[]{:S(2)}, u32[]{:S(2)}) %collective-permute-start.5) | collective-permute-done | bytes 65568 | tf_op jit(solution)/shard_map/ppermute | solution.py:77
  86.8 0.1 collective-permute-start.6
  86.9 0.6 and_select_fusion
  87.5 0.1 broadcast_in_dim.59
  87.6 0.1 broadcast_in_dim.60
  87.7 0.7 copy.31
  88.3 1.2 gather_fusion.2
  89.5 0.6 constant_dynamic-update-slice_fusion.8
  90.1 2.5 %collective-permute-done.6 = bf16[8,64,128]{2,1,0:T(8,128)(2,1)S(1)} collective-permute-done((bf16[8,64,128]{2,1,0:T(8,128)(2,1)S(1)}, bf16[8,64,128]{2,1,0:T(8,128)(2,1)S(1)}, u32[]{:S(2)}, u32[]{:S(2)}) %collective-permute-start.6) | collective-permute-done | bytes 131104 | tf_op jit(solution)/shard_map/ppermute | solution.py:77
  92.6 0.7 pad_maximum_fusion.2
  93.3 0.0 collective-permute-start.7
  93.3 0.6 constant_dynamic-update-slice_fusion.7
  94.0 0.0 collective-permute-done.2
  94.0 0.0 collective-permute-done.3
  94.0 1.0 pad_maximum_fusion.1
  95.0 0.0 copy-start.3
  95.0 0.7 gather_fusion.1
  95.7 0.7 constant_dynamic-update-slice_fusion.6
  96.4 7.1 %collective-permute-done.7 = bf16[16,64,128]{2,1,0:T(8,128)(2,1)S(1)} collective-permute-done((bf16[16,64,128]{2,1,0:T(8,128)(2,1)}, bf16[16,64,128]{2,1,0:T(8,128)(2,1)S(1)}, u32[]{:S(2)}, u32[]{:S(2)}) %collective-permute-start.7) | collective-permute-done | bytes 262176 | tf_op jit(solution)/shard_map/ppermute | solution.py:77
  103.5 0.7 constant_dynamic-update-slice_fusion.5
  104.3 0.6 constant_dynamic-update-slice_fusion.4
  104.9 0.6 constant_dynamic-update-slice_fusion.3
  105.5 0.6 constant_dynamic-update-slice_fusion.2
  106.1 0.7 constant_dynamic-update-slice_fusion.1
  106.8 0.7 constant_dynamic-update-slice_fusion
  107.5 1.1 constant_dynamic-slice_fusion
  108.6 1.1 convolution_convert_fusion.2
  109.7 1.2 fusion.11
  110.8 0.0 copy-done.5
  110.8 1.2 convolution_bitcast_fusion.1
  112.1 0.2 copy.35
  112.3 1.9 %fusion.9 = f32[16,128,256]{2,1,0:T(8,128)} fusion(bf16[16,64,256]{2,1,0:T(8,128)(2,1)S(1)} %copy-done, f32[16,64,128]{2,1,0:T(8,128)S(1)} %bitcast.57, bf16[16,64,256]{2,1,0:T(8,128)(2,1)S(1)} %copy-done.3, bf16[16,256,128]{2,1,0:T(8,128)(2,1)S(1)} %bitcast.56), kind=kOutput, calls=%fused_computation.15 | convolution fusion | flops 134479872 | bytes 4718592 | tf_op jit(solution)/shard_map/lrk,lrc->lkc/dot_general | solution.py:113
  114.2 0.0 collective-permute-done
  114.2 0.0 collective-permute-done.1
  114.2 1.7 %pad_maximum_fusion = bf16[8192,128]{1,0:T(8,128)(2,1)S(1)} fusion(bf16[2048,128]{1,0:T(8,128)(2,1)} %collective-permute-done.1, bf16[4096,128]{1,0:T(8,128)(2,1)} %param.12, bf16[2048,128]{1,0:T(8,128)(2,1)} %collective-permute-done), kind=kLoop, calls=%fused_computation.7 | loop fusion | flops 6291456 | bytes 4194304 | tf_op jit(solution)/shard_map/concatenate | solution.py:19
  115.9 6.6 %gather_fusion = bf16[128,256,128]{2,1,0:T(8,128)(2,1)} fusion(bf16[32,256,128]{2,1,0:T(8,128)(2,1)S(1)} %bitcast.52, s32[1024]{0:T(1024)S(1)} %pad_clamp_fusion.2), kind=kCustom, calls=%fused_computation | custom fusion | bytes 16777728 | tf_op jit(solution)/shard_map/gather | solution.py:53
  122.5 12.1 %copy.28 = bf16[128,256,128]{1,2,0:T(8,128)(2,1)} copy(bf16[128,256,128]{2,1,0:T(8,128)(2,1)} %gather_fusion) | data formatting | bytes 16777216 | tf_op jit(solution)/shard_map/gather | solution.py:53
  134.6 12.7 %fusion.4 = f32[16,256,128]{1,2,0:T(8,128)} fusion(f32[16,128,256]{2,1,0:T(8,128)S(1)} %copy-done.2, bf16[16,8,256,256]{3,2,1,0:T(8,128)(2,1)} %all-gather.2.cloned.1.call-done, bf16[16,8,256,128]{2,3,1,0:T(8,128)(2,1)} %bitcast.54, pred[16,8]{1,0:T(8,128)(4,1)S(1)} %iota_compare_fusion), kind=kOutput, calls=%fused_computation.9 | convolution fusion | flops 2152202240 | bytes 29360256 | tf_op jit(solution)/shard_map/lsij,lsjc->lic/dot_general | solution.py:56
  147.3 2.9 %copy.36 = f32[16,256,128]{2,1,0:T(8,128)} copy(f32[16,256,128]{1,2,0:T(8,128)} %fusion.4) | data formatting | bytes 4194304 | tf_op jit(solution)/shard_map/add | solution.py:116
  (33 shorter events, 0.2 us)
Async XLA Ops:
  6.5 1.0 copy-start
  6.5 1.4 copy-start.1
  6.5 1.7 %copy-start.4 = (bf16[2,64,512]{2,1,0:T(8,128)(2,1)S(1)}, bf16[2,64,512]{2,1,0:T(8,128)(2,1)}, u32[]{:S(2)}) copy-start(bf16[2,64,512]{2,1,0:T(8,128)(2,1)} %param.19) | copy-start | bytes 393220
  6.5 1.9 %copy-start.8 = (bf16[2,64,64]{2,1,0:T(8,128)(2,1)S(1)}, bf16[2,64,64]{2,1,0:T(8,128)(2,1)}, u32[]{:S(2)}) copy-start(bf16[2,64,64]{2,1,0:T(8,128)(2,1)} %param.22) | copy-start | bytes 49156
  6.5 128.1 %all-gather.2.cloned.1.call-start = ((), (), s32[]{:S(2)}) async-start(), calls=%async_computation | async-start | bytes 25165824 | tf_op jit(solution)/shard_map/all_gather | solution.py:50
  7.3 19.2 %copy-start.12 = (s32[2,4]{1,0:T(2,128)S(1)}, s32[2,4]{1,0:T(2,128)}, u32[]{:S(2)}) copy-start(s32[2,4]{1,0:T(2,128)} %param.21) | copy-start | bytes 100
  7.3 19.3 %copy-start.10 = (s32[16,4]{0,1:T(4,128)S(1)}, s32[16,4]{0,1:T(4,128)}, u32[]{:S(2)}) copy-start(s32[16,4]{0,1:T(4,128)} %param.18) | copy-start | bytes 772
  7.3 19.6 %copy-start.11 = (s32[16]{0:T(128)S(1)}, s32[16]{0:T(128)}, u32[]{:S(2)}) copy-start(s32[16]{0:T(128)} %param.15) | copy-start | bytes 196
  7.3 19.7 %copy-start.9 = (s32[16,8]{0,1:T(8,128)S(1)}, s32[16,8]{0,1:T(8,128)}, u32[]{:S(2)}) copy-start(s32[16,8]{0,1:T(8,128)} %param.14) | copy-start | bytes 1540
  7.3 81.0 %copy-start.7 = (bf16[4,64,256]{2,1,0:T(8,128)(2,1)S(1)}, bf16[4,64,256]{2,1,0:T(8,128)(2,1)}, u32[]{:S(2)}) copy-start(bf16[4,64,256]{2,1,0:T(8,128)(2,1)} %param.23) | copy-start | bytes 393220
  9.2 73.3 %collective-permute-start.4 = (bf16[2,64,128]{2,1,0:T(8,128)(2,1)S(1)}, bf16[2,64,128]{2,1,0:T(8,128)(2,1)S(1)}, u32[]{:S(2)}, u32[]{:S(2)}) collective-permute-start(bf16[2,64,128]{2,1,0:T(8,128)(2,1)S(1)} %get-tuple-element.10), channel_id=1, source_target_pairs={{0,30},{2,0},{4,2},{6,4},{8,6},{10,8},{12,10},{14,12},{16,14},{18,... | collective-permute-start | bytes 98312 | tf_op jit(solution)/shard_map/ppermute | solution.py:77
  16.2 77.8 %collective-permute-start.2 = (bf16[8,64,128]{2,1,0:T(8,128)(2,1)S(1)}, bf16[8,64,128]{2,1,0:T(8,128)(2,1)S(1)}, u32[]{:S(2)}, u32[]{:S(2)}) collective-permute-start(bf16[8,64,128]{2,1,0:T(8,128)(2,1)S(1)} %get-tuple-element.7), channel_id=1, source_target_pairs={{0,2},{2,4},{4,6},{6,8},{8,10},{10,12},{12,14},{14,16},{16,18},{18... | collective-permute-start | bytes 393224 | tf_op jit(solution)/shard_map/ppermute | solution.py:17
  17.5 76.5 %collective-permute-start.3 = (bf16[8,64,128]{2,1,0:T(8,128)(2,1)S(1)}, bf16[8,64,128]{2,1,0:T(8,128)(2,1)}, u32[]{:S(2)}, u32[]{:S(2)}) collective-permute-start(bf16[8,64,128]{2,1,0:T(8,128)(2,1)S(1)} %get-tuple-element.8), channel_id=1, source_target_pairs={{2,0},{4,2},{6,4},{8,6},{10,8},{12,10},{14,12},{16,14},{18,16},{20... | collective-permute-start | bytes 393224 | tf_op jit(solution)/shard_map/ppermute | solution.py:18
  19.9 94.4 %collective-permute-start = (bf16[2048,128]{1,0:T(8,128)(2,1)}, bf16[2048,128]{1,0:T(8,128)(2,1)}, u32[]{:S(2)}, u32[]{:S(2)}) collective-permute-start(bf16[2048,128]{1,0:T(8,128)(2,1)} %get-tuple-element.5), channel_id=1, source_target_pairs={{0,2},{2,4},{4,6},{6,8},{8,10},{10,12},{12,14},{14,16},{16,18},{18... | collective-permute-start | bytes 1572872 | tf_op jit(solution)/shard_map/ppermute | solution.py:17
  25.2 89.0 %collective-permute-start.1 = (bf16[2048,128]{1,0:T(8,128)(2,1)}, bf16[2048,128]{1,0:T(8,128)(2,1)}, u32[]{:S(2)}, u32[]{:S(2)}) collective-permute-start(bf16[2048,128]{1,0:T(8,128)(2,1)} %get-tuple-element.6), channel_id=1, source_target_pairs={{2,0},{4,2},{6,4},{8,6},{10,8},{12,10},{14,12},{16,14},{18,16},{20... | collective-permute-start | bytes 1572872 | tf_op jit(solution)/shard_map/ppermute | solution.py:18
  82.5 4.3 %collective-permute-start.5 = (bf16[4,64,128]{2,1,0:T(8,128)(2,1)S(1)}, bf16[4,64,128]{2,1,0:T(8,128)(2,1)S(1)}, u32[]{:S(2)}, u32[]{:S(2)}) collective-permute-start(bf16[4,64,128]{2,1,0:T(8,128)(2,1)S(1)} %pad_maximum_fusion.4), channel_id=1, source_target_pairs={{0,28},{2,30},{4,0},{6,2},{8,4},{10,6},{12,8},{14,10},{16,12},{18,... | collective-permute-start | bytes 196616 | tf_op jit(solution)/shard_map/ppermute | solution.py:77
  86.8 5.7 %collective-permute-start.6 = (bf16[8,64,128]{2,1,0:T(8,128)(2,1)S(1)}, bf16[8,64,128]{2,1,0:T(8,128)(2,1)S(1)}, u32[]{:S(2)}, u32[]{:S(2)}) collective-permute-start(bf16[8,64,128]{2,1,0:T(8,128)(2,1)S(1)} %pad_maximum_fusion.3), channel_id=1, source_target_pairs={{0,24},{2,26},{4,28},{6,30},{8,0},{10,2},{12,4},{14,6},{16,8},{18,... | collective-permute-start | bytes 393224 | tf_op jit(solution)/shard_map/ppermute | solution.py:77
  93.3 10.2 %collective-permute-start.7 = (bf16[16,64,128]{2,1,0:T(8,128)(2,1)}, bf16[16,64,128]{2,1,0:T(8,128)(2,1)S(1)}, u32[]{:S(2)}, u32[]{:S(2)}) collective-permute-start(bf16[16,64,128]{2,1,0:T(8,128)(2,1)} %pad_maximum_fusion.2), channel_id=1, source_target_pairs={{0,16},{2,18},{4,20},{6,22},{8,24},{10,26},{12,28},{14,30},{16,0},... | collective-permute-start | bytes 786440 | tf_op jit(solution)/shard_map/ppermute | solution.py:77
  94.9 14.7 %copy-start.6 = (bf16[2,64,256]{2,1,0:T(8,128)(2,1)S(1)}, bf16[2,64,256]{2,1,0:T(8,128)(2,1)}, u32[]{:S(2)}) copy-start(bf16[2,64,256]{2,1,0:T(8,128)(2,1)} %gather_fusion.2) | copy-start | bytes 196612
  95.0 15.9 %copy-start.5 = (bf16[8,64,128]{2,1,0:T(8,128)(2,1)S(1)}, bf16[8,64,128]{2,1,0:T(8,128)(2,1)}, u32[]{:S(2)}) copy-start(bf16[8,64,128]{2,1,0:T(8,128)(2,1)} %copy.31) | copy-start | bytes 393220
  95.0 17.3 %copy-start.3 = (bf16[16,64,256]{2,1,0:T(8,128)(2,1)S(1)}, bf16[16,64,256]{2,1,0:T(8,128)(2,1)}, u32[]{:S(2)}) copy-start(bf16[16,64,256]{2,1,0:T(8,128)(2,1)} %param.17) | copy-start | bytes 1572868
  122.5 12.2 %copy-start.2 = (f32[16,128,256]{2,1,0:T(8,128)S(1)}, f32[16,128,256]{2,1,0:T(8,128)}, u32[]{:S(2)}) copy-start(f32[16,128,256]{2,1,0:T(8,128)} %fusion.9) | copy-start | bytes 6291460
Sparse Core Ops, SparseCore 0:
  8.9 32.7 all-gather.1
